TPU v7x, 128 devices: a whole 4x4x4 slice. The times are simulated.
128 devices in a mesh: contour: 4 (over x), clus: 32 (over y, z, core).
Axes of the slice: x: 4, y: 4, z: 4, core: 2. Of those that a mesh axis runs over, the one named last changes fastest.
Arguments:
- probes: float32 [256, 2, 16, 128], P('clus'), may hold values from -18 to 18
- near_blocks: bfloat16 [1024, 27, 2, 128, 128], P(('contour', 'clus')), parts along dimension 0
- near_list: int32 [256, 27], P('clus'), may hold values from 0 to 255, as said below
- near_count: int32 [256], P('clus'), may hold values from 1 to 27
- cluster_rows: int32 [256], P('clus'), may hold values from 64 to 128
- row_basis: bfloat16 [1024, 2, 32, 128], P(('contour', 'clus')), parts along dimension 0, may hold values from -1 to 1
- col_basis: bfloat16 [1024, 2, 32, 128], P(('contour', 'clus')), parts along dimension 0, may hold values from -0.5 to 0.5
- far_list: int32 [256, 32], P('clus'), may hold values from 0 to 255, as said below
- far_coupling: float32 [1024, 32, 2, 32, 32], P(('contour', 'clus')), parts along dimension 0, may hold values from -0.375 to 0.375
- weight: float32 [8], P('contour'), parts along dimension 0, may hold values from -6 to 6
Outputs:
- solution: float32 [1024, 2, 16, 128], P(('contour', 'clus')), parts along dimension 0
- moment: float32 [8, 16, 16], P('contour'), parts along dimension 0
- arnoldi: float32 [16, 16], P('contour'), parts along dimension 0
There are 4 independent parts, one for each index of `contour`. A program takes and returns all parts, laid end to end along the dimension named above; an argument that names none is the same for every part. Nothing has to cross between parts.
Inputs may be any that keep to these rules, and one draw needn't show every extreme that they name: near_list[i, 0] = i; every entry lies within 8 clusters of i. `far_list`: every entry j of cluster i's list has min(|j - i|, 256 - |j - i|) > 8, so no far slot names a cluster of i's near list.
All inputs are finite; a program needn't handle non-finite values.
Results may differ from a plain program's by a relative error of at most 0.0019.
Values may be sent and summed in bfloat16 or wider, within the bound.
No kernel may reach another device: no remote copies, remote signals or barrier semaphores. Data moves between devices by JAX's collectives and lax.ppermute only.
A program may use at most 128 MiB of HBM per device.

v0:
```python
import jax
import jax.numpy as jnp
from jax import lax
from jax.sharding import PartitionSpec as P


def padded_2(cells, sides, width):
    for axis, dim in sides:
        count = lax.axis_size(axis)
        ends = count - 1
        head = lax.slice_in_dim(cells, 0, width, axis=dim)
        tail = lax.slice_in_dim(cells, cells.shape[dim] - width, cells.shape[dim], axis=dim)
        cells = jnp.concatenate(
            [
                lax.ppermute(tail, axis, [(i, (i + 1) % count) for i in range(ends)]),
                cells,
                lax.ppermute(head, axis, [((i + 1) % count, i) for i in range(ends)]),
            ],
            axis=dim,
        )
    return cells


def block_product(blocks, pulled):

    def prod(mat, vec):
        return jnp.einsum("nkrs,nkps->npr", mat, vec, preferred_element_type=jnp.float32)

    real_part = prod(blocks[:, :, 0], pulled[:, :, 0]) - prod(blocks[:, :, 1], pulled[:, :, 1])
    imag_part = prod(blocks[:, :, 0], pulled[:, :, 1]) + prod(blocks[:, :, 1], pulled[:, :, 0])
    return jnp.stack([real_part, imag_part], axis=1)


def basis_contract(basis, narrow):

    def contract(mat, vec):
        return jnp.einsum("nqr,npr->nqp", mat, vec, preferred_element_type=jnp.float32)

    real_part = contract(basis[:, 0], narrow[:, 0]) - contract(basis[:, 1], narrow[:, 1])
    imag_part = contract(basis[:, 0], narrow[:, 1]) + contract(basis[:, 1], narrow[:, 0])
    count = real_part.shape[0]
    return jnp.stack([real_part.reshape(count, -1), imag_part.reshape(count, -1)], axis=1)


def basis_expand(basis, farcoef):

    def expand(mat, vec):
        return jnp.einsum("nqr,nqp->npr", mat, vec, preferred_element_type=jnp.float32)

    real_part = expand(basis[:, 0], farcoef[:, 0]) - expand(basis[:, 1], farcoef[:, 1])
    imag_part = expand(basis[:, 0], farcoef[:, 1]) + expand(basis[:, 1], farcoef[:, 0])
    return jnp.stack([real_part, imag_part], axis=1)


def far_couple(coupling, taken):
    high = lax.Precision.HIGHEST

    def couple(mat, vec):
        return jnp.einsum("nfqs,nfsp->nqp", mat, vec, precision=high)

    real_part = couple(coupling[:, :, 0], taken[:, :, 0]) - couple(
        coupling[:, :, 1], taken[:, :, 1]
    )
    imag_part = couple(coupling[:, :, 0], taken[:, :, 1]) + couple(
        coupling[:, :, 1], taken[:, :, 0]
    )
    return jnp.stack([real_part, imag_part], axis=1)


def inner(left, right):
    real_part = jnp.sum(left[:, 0] * right[:, 0] + left[:, 1] * right[:, 1], axis=(0, 2))
    imag_part = jnp.sum(left[:, 0] * right[:, 1] - left[:, 1] * right[:, 0], axis=(0, 2))
    return (real_part, imag_part)


def squares(field):
    return jnp.sum(field * field, axis=(0, 1, 3))


def scaled(field, real_part, imag_part):
    sr = real_part[None, :, None]
    si = imag_part[None, :, None]
    return jnp.stack(
        [sr * field[:, 0] - si * field[:, 1], sr * field[:, 1] + si * field[:, 0]], axis=1
    )


def shards(
    probes,
    near_blocks,
    near_list,
    near_count,
    cluster_rows,
    row_basis,
    col_basis,
    far_list,
    far_coupling,
    weight,
):
    owned = probes.shape[0]
    nprobe = probes.shape[2]
    width = probes.shape[3]
    rank = col_basis.shape[2]
    first_id = lax.axis_index("clus") * owned
    total_clusters = owned * lax.axis_size("clus")
    rows_iota = lax.broadcasted_iota(jnp.int32, (owned, width), 1)
    row_mask = (rows_iota < cluster_rows[:, None]).astype(jnp.float32)[:, None, None, :]
    slots_iota = lax.broadcasted_iota(jnp.int32, near_list.shape, 1)
    slot_live = slots_iota < near_count[:, None]
    local_ids = near_list - (first_id - owned)

    def operate(field):
        narrow = field.astype(jnp.bfloat16)
        padded = padded_2(narrow, (("clus", 0),), owned)
        pulled = jnp.take(padded, local_ids, axis=0)
        pulled = jnp.where(slot_live[:, :, None, None, None], pulled, jnp.zeros((), jnp.bfloat16))
        near = block_product(near_blocks, pulled)
        coef = basis_contract(col_basis, narrow)
        whole = lax.all_gather(coef, "clus", axis=0, tiled=True)
        whole = whole.reshape(whole.shape[0], 2, rank, nprobe)
        taken = jnp.take(whole, far_list, axis=0)
        farcoef = far_couple(far_coupling, taken)
        farcoef_b = farcoef.astype(jnp.bfloat16)
        far = basis_expand(row_basis, farcoef_b)
        return (near + far) * row_mask

    base = probes * row_mask
    beta = jnp.sqrt(lax.psum(squares(base), "clus") + 1e-06)
    first = base / beta[None, None, :, None]
    image_one = operate(first)
    local_re, local_im = inner(first, image_one)
    proj_re, proj_im = lax.psum((local_re, local_im), "clus")
    remain = image_one - scaled(first, proj_re, proj_im)
    norm_sq = lax.psum(squares(remain), "clus")
    size_two = jnp.sqrt(norm_sq + 1e-06)
    second = remain / size_two[None, None, :, None]
    factor = 1.0 / (total_clusters * width)
    arnoldi = jnp.stack([beta * jnp.sqrt(jnp.float32(factor)), proj_re, proj_im, size_two], axis=0)
    image_two = operate(second)
    g12r, g12i = inner(image_one, image_two)
    q1r, q1i = inner(image_one, base)
    q2r, q2i = inner(image_two, base)
    g11, g22, g12r, g12i, q1r, q1i, q2r, q2i = lax.psum(
        (squares(image_one), squares(image_two), g12r, g12i, q1r, q1i, q2r, q2i), "clus"
    )
    det = g11 * g22 - (g12r * g12r + g12i * g12i)
    y1r = (g22 * q1r - (g12r * q2r - g12i * q2i)) / det
    y1i = (g22 * q1i - (g12r * q2i + g12i * q2r)) / det
    y2r = (g11 * q2r - (g12r * q1r + g12i * q1i)) / det
    y2i = (g11 * q2i - (g12r * q1i - g12i * q1r)) / det
    iterate = scaled(first, y1r, y1i) + scaled(second, y2r, y2i)
    wr = weight[0]
    wi = weight[1]
    solution = jnp.stack(
        [wr * iterate[:, 0] - wi * iterate[:, 1], wr * iterate[:, 1] + wi * iterate[:, 0]], axis=1
    )
    high = lax.Precision.HIGHEST
    mom_re = jnp.einsum("npr,nqr->pq", base[:, 0], iterate[:, 0], precision=high) + jnp.einsum(
        "npr,nqr->pq", base[:, 1], iterate[:, 1], precision=high
    )
    mom_im = jnp.einsum("npr,nqr->pq", base[:, 0], iterate[:, 1], precision=high) - jnp.einsum(
        "npr,nqr->pq", base[:, 1], iterate[:, 0], precision=high
    )
    mom_re, mom_im = lax.psum((mom_re, mom_im), "clus")
    moment = jnp.stack([wr * mom_re - wi * mom_im, wr * mom_im + wi * mom_re], axis=0) * factor
    return (solution, moment, arnoldi)


def solution(mesh):
    in_specs = (
        P("clus", None, None, None),
        P(("contour", "clus"), None, None, None, None),
        P("clus", None),
        P("clus"),
        P("clus"),
        P(("contour", "clus"), None, None, None),
        P(("contour", "clus"), None, None, None),
        P("clus", None),
        P(("contour", "clus"), None, None, None, None),
        P("contour"),
    )
    out_specs = (
        P(("contour", "clus"), None, None, None),
        P("contour", None, None),
        P("contour", None),
    )
    return jax.shard_map(shards, mesh=mesh, in_specs=in_specs, out_specs=out_specs, check_vma=False)
```

profile of v0, /device:TPU:0, one launch (start us, length us, event | category | flops | bytes accessed | tf_op | source)
XLA Modules:
  0.0 565.3 jit_solution(2159509121463575209)
XLA Ops:
  9.0 68.7 %psum.98 = f32[16]{0:T(128)S(1)} all-reduce(f32[16]{0:T(128)S(1)} %get-tuple-element.43), channel_id=1, replica_groups=mesh['contour'=4,'clus'=32] {'clus'}, use_global_device_ids=true, to_apply=%region_1.0 | all-reduce | flops 16 | bytes 128 | tf_op jit(solution)/shard_map/psum | solution.py:128
  79.1 3.0 collective-permute-start
  92.9 5.5 fusion.51
  99.0 2.0 fusion.48
  101.0 2.0 fusion.119
  103.0 2.0 fusion.125
  105.1 21.4 %all-gather.3.cloned.1.call-done = f32[256,2,512]{2,0,1:T(8,128)} async-done(((f32[8,2,512]{2,0,1:T(8,128)}), f32[256,2,512]{2,0,1:T(8,128)}) %all-gather.3.cloned.1.call-update) | async-done | bytes 1048592 | tf_op jit(solution)/shard_map/all_gather | solution.py:119
  128.0 4.4 copy.34
  132.4 5.0 gather_fusion.1
  137.4 2.6 copy.35
  142.4 3.7 fusion.83
  146.1 3.7 fusion.80
  149.8 3.7 fusion.143
  153.6 3.9 fusion.140
  158.2 65.2 %all-reduce.2 = (f32[16]{0:T(128)S(1)}, f32[16]{0:T(128)S(1)}) all-reduce(f32[16]{0:T(128)S(1)} %get-tuple-element.18, f32[16]{0:T(128)S(1)} %get-tuple-element.17), channel_id=1, replica_groups=mesh['contour'=4,'clus'=32] {'clus'}, use_global_device_ids=true, to_apply=%region_5.8 | all-reduce | flops 32 | bytes 256 | tf_op jit(solution)/shard_map/psum | solution.py:132
  223.6 62.7 %psum.101 = f32[16]{0:T(128)S(1)} all-reduce(f32[16]{0:T(128)S(1)} %get-tuple-element.22), channel_id=1, replica_groups=mesh['contour'=4,'clus'=32] {'clus'}, use_global_device_ids=true, to_apply=%region_7.10 | all-reduce | flops 16 | bytes 128 | tf_op jit(solution)/shard_map/psum | solution.py:134
  288.0 3.0 collective-permute-start.2
  295.1 5.2 fusion.57
  300.3 5.2 fusion.54
  305.5 5.2 fusion.107
  310.7 2.0 fusion.113
  312.7 19.7 %all-gather.5.cloned.1.call-done = f32[256,2,512]{2,0,1:T(8,128)} async-done(((f32[8,2,512]{2,0,1:T(8,128)}), f32[256,2,512]{2,0,1:T(8,128)}) %all-gather.5.cloned.1.call-update) | async-done | bytes 1048592 | tf_op jit(solution)/shard_map/all_gather | solution.py:119
  333.9 4.4 copy.44
  338.3 5.0 gather_fusion.3
  343.3 2.6 copy.45
  346.7 1.6 slice-done.3
  348.3 3.7 fusion.89
  352.0 3.7 fusion.86
  355.8 3.7 fusion.149
  359.6 4.0 fusion.146
  364.4 65.2 %all-reduce.1 = (f32[16]{0:T(128)S(1)}, f32[16]{0:T(128)S(1)}, f32[16]{0:T(128)S(1)}, f32[16]{0:T(128)S(1)}, f32[16]{0:T(128)S(1)}, /*index=5*/f32[16]{0:T(128)S(1)}, f32[16]{0:T(128)S(1)}, f32[16]{0:T(128)S(1)}) all-reduce(f32[16]{0:T(128)S(1)} %get-tuple-element.45, ...), channel_id=1, replica_groups=mesh['contour'=4,'clus'=32] {'clus'}, use_global_device_ids=true, to_apply=%region_17.20 | all-reduce | flops 128 | bytes 1024 | tf_op jit(solution)/shard_map/psum | solution.py:143
  432.6 123.8 %all-reduce = (f32[16,16]{1,0:T(8,128)S(1)}, f32[16,16]{1,0:T(8,128)S(1)}) all-reduce(f32[16,16]{1,0:T(8,128)S(1)} %fusion.152, f32[16,16]{1,0:T(8,128)S(1)} %fusion.153), channel_id=1, replica_groups=mesh['contour'=4,'clus'=32] {'clus'}, use_global_device_ids=true, to_apply=%region_24.27 | all-reduce | flops 512 | bytes 4096 | tf_op jit(solution)/shard_map/psum | solution.py:164
  (106 shorter events, 33.1 us)
Async XLA Ops:
  7.2 119.3 %all-gather.3.cloned.1.call-start = ((), (), s32[]{:S(2)}) async-start(), calls=%async_computation | async-start | bytes 1081344 | tf_op jit(solution)/shard_map/all_gather | solution.py:119
  77.8 13.1 %collective-permute-start.1 = (bf16[8,2,16,128]{3,2,0,1:T(8,128)(2,1)S(1)}, bf16[8,2,16,128]{3,2,0,1:T(8,128)(2,1)S(1)}, u32[]{:S(2)}, u32[]{:S(2)}) collective-permute-start(bf16[8,2,16,128]{3,2,0,1:T(8,128)(2,1)S(1)} %get-tuple-element.41), channel_id=1, source_target_pairs={{1,0},{2,1},{3,2},{4,3},{5,4},{6,5},{7,6},{8,7},{9,8},{10,9},{11,1... | collective-permute-start | bytes 196616 | tf_op jit(solution)/shard_map/ppermute | solution.py:17
  79.1 11.8 %collective-permute-start = (bf16[8,2,16,128]{3,2,0,1:T(8,128)(2,1)S(1)}, bf16[8,2,16,128]{3,2,0,1:T(8,128)(2,1)S(1)}, u32[]{:S(2)}, u32[]{:S(2)}) collective-permute-start(bf16[8,2,16,128]{3,2,0,1:T(8,128)(2,1)S(1)} %get-tuple-element.41), channel_id=1, source_target_pairs={{0,1},{1,2},{2,3},{3,4},{4,5},{5,6},{6,7},{7,8},{8,9},{9,10},{10,1... | collective-permute-start | bytes 196616 | tf_op jit(solution)/shard_map/ppermute | solution.py:15
  87.2 245.2 %all-gather.5.cloned.1.call-start = ((), (), s32[]{:S(2)}) async-start(), calls=%async_computation.1 | async-start | bytes 1081344 | tf_op jit(solution)/shard_map/all_gather | solution.py:119
  91.9 7.1 %copy-start.2 = (bf16[8,27,2,128,128]{4,3,2,1,0:T(8,128)(2,1)S(1)}, bf16[8,27,2,128,128]{4,3,2,1,0:T(8,128)(2,1)}, u32[]{:S(2)}) copy-start(bf16[8,27,2,128,128]{4,3,2,1,0:T(8,128)(2,1)} %param.15) | copy-start | bytes 42467332
  137.3 3.7 slice-start
  140.0 2.4 slice-start.1
  153.5 3.9 copy-start.1
  153.6 132.8 %copy-start = (bf16[8,2,32,128]{3,2,1,0:T(8,128)(2,1)S(1)}, bf16[8,2,32,128]{3,2,1,0:T(8,128)(2,1)}, u32[]{:S(2)}) copy-start(bf16[8,2,32,128]{3,2,1,0:T(8,128)(2,1)} %param.20) | copy-start | bytes 393220
  286.7 6.3 %collective-permute-start.3 = (bf16[8,2,16,128]{3,2,0,1:T(8,128)(2,1)S(1)}, bf16[8,2,16,128]{3,2,0,1:T(8,128)(2,1)S(1)}, u32[]{:S(2)}, u32[]{:S(2)}) collective-permute-start(bf16[8,2,16,128]{3,2,0,1:T(8,128)(2,1)S(1)} %get-tuple-element.37), channel_id=1, source_target_pairs={{1,0},{2,1},{3,2},{4,3},{5,4},{6,5},{7,6},{8,7},{9,8},{10,9},{11,1... | collective-permute-start | bytes 196616 | tf_op jit(solution)/shard_map/ppermute | solution.py:17
  288.0 5.0 collective-permute-start.2
  295.0 15.6 %slice-start.4 = ((s8[14155776]{0:T(1024)(128)(4,1)}), s8[4194304]{0:T(1024)(128)(4,1)S(1)}, s32[]{:S(2)}) async-start(s8[14155776]{0:T(1024)(128)(4,1)} %bitcast.486), calls=%async_computation.6 | async-start | bytes 8388608
  295.1 15.6 %slice-start.5 = ((s8[14155776]{0:T(1024)(128)(4,1)}), s8[4194304]{0:T(1024)(128)(4,1)S(1)}, s32[]{:S(2)}) async-start(s8[14155776]{0:T(1024)(128)(4,1)} %bitcast.486), calls=%async_computation.7 | async-start | bytes 8388608
  300.2 10.4 %slice-start.6 = ((s8[14155776]{0:T(1024)(128)(4,1)}), s8[4194304]{0:T(1024)(128)(4,1)S(1)}, s32[]{:S(2)}) async-start(s8[14155776]{0:T(1024)(128)(4,1)} %bitcast.486), calls=%async_computation.8 | async-start | bytes 8388608
  305.4 5.2 slice-start.7
  343.3 3.4 slice-start.2
  345.9 2.4 slice-start.3
Sparse Core Ops, SparseCore 0:
  87.3 39.0 all-gather.2
  292.6 39.7 all-gather.4
where the time goes:
time: 572 us; the launch traced here: 565 us
  blocking collectives  386 us (67%)
  matrix products  65.8 us (12%)
  waiting for transfers between devices  41.1 us (7%)
  local copies, waits for them, and re-layouts  36.3 us (6%)
  between operations  14.7 us (3%)
  other arithmetic  13.1 us (2%)
  starting transfers between devices  8.74 us (2%)
    psum x1, blocking collectives, shards(): mom_re, mom_im = lax.psum((mom_re, mom_im), 'clus')  124 us
    psum x1, blocking collectives, shards(): beta = jnp.sqrt(lax.psum(squares(base), 'clus') + 1e-06)  68.7 us
    psum x1, blocking collectives, shards(): lax.psum((squares(image_one), squares(image_two), g12r, g12i, q1r, q1i, q...  65.2 us
    psum x1, blocking collectives, shards(): proj_re, proj_im = lax.psum((local_re, local_im), 'clus')  65.2 us
    psum x1, blocking collectives, shards(): norm_sq = lax.psum(squares(remain), 'clus')  62.7 us
    all_gather x2, waiting for transfers between devices, operate(): whole = lax.all_gather(coef, 'clus', axis=0, tiled=True)  41 us
    dot_general x8, matrix products, couple(): return jnp.einsum('nfqs,nfsp->nqp', mat, vec, precision=high)  30.2 us
    dot_general x8, matrix products, prod(): jnp.einsum('nkrs,nkps->npr', mat, vec, preferred_element_type=jnp.float32)  29.1 us
  transfers between devices with their start and end apart: 6, of which 2 were waited for; matrix products, arithmetic and copies ran while one was open for 8% of the time, Pallas kernels for 0%

commit v1 on v0

--- a/solution.py
+++ b/solution.py
@@ -116,7 +116,10 @@
         pulled = jnp.where(slot_live[:, :, None, None, None], pulled, jnp.zeros((), jnp.bfloat16))
         near = block_product(near_blocks, pulled)
         coef = basis_contract(col_basis, narrow)
-        whole = lax.all_gather(coef, "clus", axis=0, tiled=True)
+        peers = lax.axis_size("clus")
+        pieces = jnp.stack([coef for _ in range(peers)])
+        pieces = lax.all_to_all(pieces, "clus", split_axis=0, concat_axis=0)
+        whole = jnp.concatenate(pieces, axis=0)
         whole = whole.reshape(whole.shape[0], 2, rank, nprobe)
         taken = jnp.take(whole, far_list, axis=0)
         farcoef = far_couple(far_coupling, taken)

time: 572 us -> 543 us (0.949)
  waiting for transfers between devices: 41.1 us -> 1.72 us
  local copies, waits for them, and re-layouts: 36.3 us -> 49.6 us
  between operations: 14.7 us -> 1.5 us
  starting transfers between devices: 8.74 us -> 16.5 us
    all_gather x2 -> x0, waiting for transfers between devices: 41 us -> none  [operate(): whole = lax.all_gather(coef, 'clus', axis=0, tiled=True)]
    another operation x0 -> x6, local copies, waits for them, and re-layouts: none -> 25.6 us  [the longest x4 23.4 us: operate(): whole = whole.reshape(whole.shape[0], 2, rank, nprobe)]
    reshape x2 -> x0, local copies, waits for them, and re-layouts: 8.75 us -> none  [operate(): whole = whole.reshape(whole.shape[0], 2, rank, nprobe)]
    all_to_all x0 -> x2, starting transfers between devices: none -> 7.86 us  [operate(): pieces = lax.all_to_all(pieces, 'clus', split_axis=0, concat_axis=0)]
  transfers between devices with their start and end apart: 6 -> 6, of which waited for: 2 -> 1; matrix products, arithmetic and copies ran while one was open for 8% -> 8% of each run, Pallas kernels for 0% -> 0%
where the time goes in v1:
time: 543 us; the launch traced here: 536 us
  blocking collectives  389 us (72%)
  matrix products  65.6 us (12%)
  local copies, waits for them, and re-layouts  49.6 us (9%)
  starting transfers between devices  16.5 us (3%)
  other arithmetic  12.4 us (2%)
    psum x1, blocking collectives, shards(): mom_re, mom_im = lax.psum((mom_re, mom_im), 'clus')  124 us
    psum x1, blocking collectives, shards(): beta = jnp.sqrt(lax.psum(squares(base), 'clus') + 1e-06)  68.7 us
    psum x1, blocking collectives, shards(): lax.psum((squares(image_one), squares(image_two), g12r, g12i, q1r, q1i, q...  67.6 us
    psum x1, blocking collectives, shards(): proj_re, proj_im = lax.psum((local_re, local_im), 'clus')  65.9 us
    psum x1, blocking collectives, shards(): norm_sq = lax.psum(squares(remain), 'clus')  62.7 us
    dot_general x8, matrix products, couple(): return jnp.einsum('nfqs,nfsp->nqp', mat, vec, precision=high)  30.2 us
    dot_general x8, matrix products, prod(): jnp.einsum('nkrs,nkps->npr', mat, vec, preferred_element_type=jnp.float32)  29 us
    another operation x4, local copies, waits for them, and re-layouts, operate(): whole = whole.reshape(whole.shape[0], 2, rank, nprobe)  23.4 us
  transfers between devices with their start and end apart: 6, of which 1 were waited for; matrix products, arithmetic and copies ran while one was open for 8% of the time, Pallas kernels for 0%

profile of v1, /device:TPU:0, one launch (start us, length us, event | category | flops | bytes accessed | tf_op | source)
XLA Modules:
  0.0 536.0 jit_solution(11849020375329644086)
XLA Ops:
  2.5 68.7 %psum.98 = f32[16]{0:T(128)S(1)} all-reduce(f32[16]{0:T(128)S(1)} %get-tuple-element.46), channel_id=1, replica_groups=mesh['contour'=4,'clus'=32] {'clus'}, use_global_device_ids=true, to_apply=%region_1.0 | all-reduce | flops 16 | bytes 128 | tf_op jit(solution)/shard_map/psum | solution.py:131
  73.1 3.0 collective-permute-start
  81.7 3.9 all-to-all-start
  88.6 5.4 %fusion.51 = f32[8,16,128]{2,1,0:T(8,128)S(1)} fusion(bf16[8,27,2,128,128]{4,3,2,1,0:T(8,128)(2,1)} %param.15, bf16[8,27,2,16,128]{4,3,1,0,2:T(8,128)(2,1)S(1)} %select_select_fusion.1), kind=kOutput, calls=%fused_computation.61 | convolution fusion | flops 113246208 | bytes 8028160 | tf_op jit(solution)/shard_map/nkrs,nkps->npr/dot_general | solution.py:27
  94.6 2.0 fusion.119
  96.6 2.0 fusion.48
  98.6 2.0 fusion.125
  102.4 4.9 reshape_reshape.6
  107.3 6.8 %copy.54 = f32[256,2,32,16]{2,3,1,0:T(8,128)} copy(f32[256,2,32,16]{3,2,0,1:T(8,128)} %reshape_reshape.6) | data formatting | bytes 2097152 | tf_op jit(solution)/shard_map/reshape;reshape | solution.py:123
  114.2 4.9 gather_fusion.1
  119.1 2.6 copy.55
  124.1 3.7 fusion.83
  127.8 3.7 fusion.80
  131.6 3.7 fusion.143
  135.3 3.9 fusion.140
  140.0 65.9 %all-reduce.2 = (f32[16]{0:T(128)S(1)}, f32[16]{0:T(128)S(1)}) all-reduce(f32[16]{0:T(128)S(1)} %get-tuple-element.21, f32[16]{0:T(128)S(1)} %get-tuple-element.20), channel_id=1, replica_groups=mesh['contour'=4,'clus'=32] {'clus'}, use_global_device_ids=true, to_apply=%region_5.8 | all-reduce | flops 32 | bytes 256 | tf_op jit(solution)/shard_map/psum | solution.py:135
  206.6 62.7 %psum.101 = f32[16]{0:T(128)S(1)} all-reduce(f32[16]{0:T(128)S(1)} %get-tuple-element.25), channel_id=1, replica_groups=mesh['contour'=4,'clus'=32] {'clus'}, use_global_device_ids=true, to_apply=%region_7.10 | all-reduce | flops 16 | bytes 128 | tf_op jit(solution)/shard_map/psum | solution.py:137
  271.6 3.0 collective-permute-start.2
  276.5 3.9 all-to-all-start.1
  283.8 5.2 fusion.57
  289.0 5.2 fusion.107
  294.2 5.2 fusion.54
  301.5 4.9 reshape_reshape.7
  306.4 6.8 %copy.64 = f32[256,2,32,16]{2,3,1,0:T(8,128)} copy(f32[256,2,32,16]{3,2,0,1:T(8,128)} %reshape_reshape.7) | data formatting | bytes 2097152 | tf_op jit(solution)/shard_map/reshape;reshape | solution.py:123
  313.2 4.9 gather_fusion.3
  318.1 2.6 copy.65
  323.2 3.7 fusion.89
  326.9 3.7 fusion.86
  330.6 3.7 fusion.149
  334.5 4.0 fusion.146
  339.3 67.6 %all-reduce.1 = (f32[16]{0:T(128)S(1)}, f32[16]{0:T(128)S(1)}, f32[16]{0:T(128)S(1)}, f32[16]{0:T(128)S(1)}, f32[16]{0:T(128)S(1)}, /*index=5*/f32[16]{0:T(128)S(1)}, f32[16]{0:T(128)S(1)}, f32[16]{0:T(128)S(1)}) all-reduce(f32[16]{0:T(128)S(1)} %get-tuple-element.48, ...), channel_id=1, replica_groups=mesh['contour'=4,'clus'=32] {'clus'}, use_global_device_ids=true, to_apply=%region_17.20 | all-reduce | flops 128 | bytes 1024 | tf_op jit(solution)/shard_map/psum | solution.py:146
  410.0 123.8 %all-reduce = (f32[16,16]{1,0:T(8,128)S(1)}, f32[16,16]{1,0:T(8,128)S(1)}) all-reduce(f32[16,16]{1,0:T(8,128)S(1)} %fusion.152, f32[16,16]{1,0:T(8,128)S(1)} %fusion.153), channel_id=1, replica_groups=mesh['contour'=4,'clus'=32] {'clus'}, use_global_device_ids=true, to_apply=%region_24.27 | all-reduce | flops 512 | bytes 4096 | tf_op jit(solution)/shard_map/psum | solution.py:167
  (126 shorter events, 36.1 us)
Async XLA Ops:
  0.6 85.0 %copy-start.3 = (s32[8,32]{1,0:T(8,128)S(1)}, s32[8,32]{1,0:T(8,128)}, u32[]{:S(2)}) copy-start(s32[8,32]{1,0:T(8,128)} %param.21) | copy-start | bytes 3076
  0.6 85.0 %copy-start.6 = (s32[8,27]{1,0:T(8,128)S(1)}, s32[8,27]{1,0:T(8,128)}, u32[]{:S(2)}) copy-start(s32[8,27]{1,0:T(8,128)} %param.16) | copy-start | bytes 2596
  0.7 85.0 %copy-start.9 = (s32[8]{0:T(128)S(1)}, s32[8]{0:T(128)}, u32[]{:S(2)}) copy-start(s32[8]{0:T(128)} %param.17) | copy-start | bytes 100
  0.7 85.2 %copy-start.8 = (f32[2]{0:T(128)S(1)}, f32[2]{0:T(128)}, u32[]{:S(2)}) copy-start(f32[2]{0:T(128)} %param.23) | copy-start | bytes 28
  71.8 14.8 %collective-permute-start.1 = (bf16[8,2,16,128]{3,2,0,1:T(8,128)(2,1)S(1)}, bf16[8,2,16,128]{3,2,0,1:T(8,128)(2,1)S(1)}, u32[]{:S(2)}, u32[]{:S(2)}) collective-permute-start(bf16[8,2,16,128]{3,2,0,1:T(8,128)(2,1)S(1)} %get-tuple-element.44), channel_id=1, source_target_pairs={{1,0},{2,1},{3,2},{4,3},{5,4},{6,5},{7,6},{8,7},{9,8},{10,9},{11,1... | collective-permute-start | bytes 196616 | tf_op jit(solution)/shard_map/ppermute | solution.py:17
  73.1 13.5 %collective-permute-start = (bf16[8,2,16,128]{3,2,0,1:T(8,128)(2,1)S(1)}, bf16[8,2,16,128]{3,2,0,1:T(8,128)(2,1)S(1)}, u32[]{:S(2)}, u32[]{:S(2)}) collective-permute-start(bf16[8,2,16,128]{3,2,0,1:T(8,128)(2,1)S(1)} %get-tuple-element.44), channel_id=1, source_target_pairs={{0,1},{1,2},{2,3},{3,4},{4,5},{5,6},{6,7},{7,8},{8,9},{9,10},{10,1... | collective-permute-start | bytes 196616 | tf_op jit(solution)/shard_map/ppermute | solution.py:15
  81.7 20.7 %all-to-all-start = ((f32[32,8,2,512]{3,1,2,0:T(8,128)}), f32[32,8,2,512]{3,1,2,0:T(8,128)S(1)}, u32[]{:S(2)}, u32[]{:S(2)}) async-start(f32[32,8,2,512]{3,1,2,0:T(8,128)} %stack.66), calls=%async_computation | async-start | bytes 2097152 | tf_op jit(solution)/shard_map/all_to_all | solution.py:121
  85.7 2.8 copy-start.4
  85.7 2.8 copy-start.5
  87.6 7.1 %copy-start.11 = (bf16[8,27,2,128,128]{4,3,2,1,0:T(8,128)(2,1)S(1)}, bf16[8,27,2,128,128]{4,3,2,1,0:T(8,128)(2,1)}, u32[]{:S(2)}) copy-start(bf16[8,27,2,128,128]{4,3,2,1,0:T(8,128)(2,1)} %param.15) | copy-start | bytes 42467332
  119.1 3.7 slice-start
  121.7 2.4 slice-start.1
  135.3 3.9 copy-start.1
  135.3 134.7 %copy-start = (bf16[8,2,32,128]{3,2,1,0:T(8,128)(2,1)S(1)}, bf16[8,2,32,128]{3,2,1,0:T(8,128)(2,1)}, u32[]{:S(2)}) copy-start(bf16[8,2,32,128]{3,2,1,0:T(8,128)(2,1)} %param.20) | copy-start | bytes 393220
  139.2 141.2 %copy-start.10 = (f32[1,16]{1,0:T(1,128)S(1)}, f32[1,16]{1,0:T(1,128)}, u32[]{:S(2)}) copy-start(f32[1,16]{1,0:T(1,128)} %get-tuple-element.64) | copy-start | bytes 196
  270.3 10.8 %collective-permute-start.3 = (bf16[8,2,16,128]{3,2,0,1:T(8,128)(2,1)S(1)}, bf16[8,2,16,128]{3,2,0,1:T(8,128)(2,1)S(1)}, u32[]{:S(2)}, u32[]{:S(2)}) collective-permute-start(bf16[8,2,16,128]{3,2,0,1:T(8,128)(2,1)S(1)} %get-tuple-element.40), channel_id=1, source_target_pairs={{1,0},{2,1},{3,2},{4,3},{5,4},{6,5},{7,6},{8,7},{9,8},{10,9},{11,1... | collective-permute-start | bytes 196616 | tf_op jit(solution)/shard_map/ppermute | solution.py:17
  271.6 9.4 %collective-permute-start.2 = (bf16[8,2,16,128]{3,2,0,1:T(8,128)(2,1)S(1)}, bf16[8,2,16,128]{3,2,0,1:T(8,128)(2,1)S(1)}, u32[]{:S(2)}, u32[]{:S(2)}) collective-permute-start(bf16[8,2,16,128]{3,2,0,1:T(8,128)(2,1)S(1)} %get-tuple-element.40), channel_id=1, source_target_pairs={{0,1},{1,2},{2,3},{3,4},{4,5},{5,6},{6,7},{7,8},{8,9},{9,10},{10,1... | collective-permute-start | bytes 196616 | tf_op jit(solution)/shard_map/ppermute | solution.py:15
  276.5 24.9 %all-to-all-start.1 = ((f32[32,8,2,512]{3,1,2,0:T(8,128)}), f32[32,8,2,512]{3,1,2,0:T(8,128)S(1)}, u32[]{:S(2)}, u32[]{:S(2)}) async-start(f32[32,8,2,512]{3,1,2,0:T(8,128)} %stack.75), calls=%async_computation.1 | async-start | bytes 2097152 | tf_op jit(solution)/shard_map/all_to_all | solution.py:121
  283.8 15.6 %slice-start.4 = ((s8[14155776]{0:T(1024)(128)(4,1)}), s8[4194304]{0:T(1024)(128)(4,1)S(1)}, s32[]{:S(2)}) async-start(s8[14155776]{0:T(1024)(128)(4,1)} %bitcast.490), calls=%async_computation.6 | async-start | bytes 8388608
  283.8 15.6 %slice-start.5 = ((s8[14155776]{0:T(1024)(128)(4,1)}), s8[4194304]{0:T(1024)(128)(4,1)S(1)}, s32[]{:S(2)}) async-start(s8[14155776]{0:T(1024)(128)(4,1)} %bitcast.490), calls=%async_computation.7 | async-start | bytes 8388608
  289.0 10.4 %slice-start.6 = ((s8[14155776]{0:T(1024)(128)(4,1)}), s8[4194304]{0:T(1024)(128)(4,1)S(1)}, s32[]{:S(2)}) async-start(s8[14155776]{0:T(1024)(128)(4,1)} %bitcast.490), calls=%async_computation.8 | async-start | bytes 8388608
  294.2 5.2 slice-start.7
  318.1 3.4 slice-start.2
  320.8 2.4 slice-start.3
  334.3 4.9 copy-start.7
  334.3 72.6 %copy-start.2 = (f32[8,2,16,128]{3,2,0,1:T(8,128)S(1)}, f32[8,2,16,128]{3,2,0,1:T(8,128)}, u32[]{:S(2)}) copy-start(f32[8,2,16,128]{3,2,0,1:T(8,128)} %get-tuple-element.41) | copy-start | bytes 393220
